TPU v7x, 512 devices: a whole 4x8x8 slice. The times are simulated.
512 devices in a mesh: cells: 32 (over y, x), genes: 16 (over z, core).
Axes of the slice: x: 4, y: 8, z: 8, core: 2. Of those that a mesh axis runs over, the one named last changes fastest.
Arguments:
- counts: int32 [32768, 4096], P('cells', 'genes'), may hold values from 0 to 128, as said below
- batch: int32 [32768, 1], P(('cells', 'genes')), may hold values from 0 to 63
- seeds: int32 [32768, 1], P(('cells', 'genes')), may hold values from 0 to 1023
- loadings: bfloat16 [4096, 256], P('genes'), may hold values from -0.09375 to 0.09375
Outputs:
- embedding: float32 [32768, 256], P(('cells', 'genes'))
- assign: float32 [32768, 1024], P(('cells', 'genes'))
- centroids: bfloat16 [1024, 256], replicated
Inputs may be any that keep to these rules, and one draw needn't show every extreme that they name: counts[i, g] >= 1 wherever g mod 64 equals i mod 64. `batch`: every label occurs. `seeds`: every cluster is the seed of some cell.
All inputs are finite; a program needn't handle non-finite values.
Results may differ from a plain program's by a relative error of at most 0.012.
The roundings to bfloat16 on the way count: a program that leaves them out, or rounds other values in their place, can miss the bound.
Values may be sent and summed in bfloat16 or wider, within the bound.
No kernel may reach another device: no remote copies, remote signals or barrier semaphores. Data moves between devices by JAX's collectives and lax.ppermute only.
A program may use at most 64 MiB of HBM per device.

v0:
```python
import jax
import jax.numpy as jnp
from jax import lax
from jax.sharding import PartitionSpec as P

K = 1024
B = 64
ITERS = 2
X_SIZE = 4
Y_AXIS = "y"
X_AXIS = "x"
CELL_AXIS = (Y_AXIS, X_AXIS)
Z_AXIS = "z"
CORE_AXIS = "core"
GENE_AXIS = (Z_AXIS, CORE_AXIS)
epsilon = 1e-06
cluster_spread = 0.1
f32 = jnp.float32
bf16 = jnp.bfloat16
trailing = (((1,), (1,)), ((), ()))
together = lax.optimization_barrier


def exchange(blocks, axis):
    return lax.all_to_all(blocks, axis, 0, 0, tiled=False)


def share(block, axis):
    return exchange(jnp.broadcast_to(block[None], (lax.axis_size(axis),) + block.shape), axis)


def gather(block, axis):
    return lax.all_gather(block, axis, tiled=True)


def dot(left, right):
    return jnp.dot(left, right, preferred_element_type=f32)


def dot_rows(left, right):
    return lax.dot_general(left, right, trailing, preferred_element_type=f32)


def hot_columns(labels, count):
    return (labels[None, :] == jnp.arange(count, dtype=f32)[:, None]).astype(bf16)


def halves(value):
    high = value.astype(bf16)
    return (high, (value - high.astype(f32)).astype(bf16))


def unit(rows):
    scaled = rows * lax.rsqrt(jnp.sum(rows * rows, axis=1, keepdims=True) + epsilon)
    return scaled.astype(bf16)


def penalty_halves(observed, batch_total, total_cells):
    mass = jnp.sum(observed, axis=1, keepdims=True)
    ratio = (mass * batch_total / total_cells + 1.0) / (observed + 1.0)
    return jnp.concatenate(halves(ratio * ratio), axis=1)


def added(blocks):
    total = blocks[0].astype(f32)
    for at in range(1, blocks.shape[0]):
        total = total + blocks[at].astype(f32)
    return total


def folded(observed):
    half = observed.shape[0] // 2
    return jnp.concatenate([observed[:half], observed[half:]], axis=1).astype(bf16)


def everywhere(sums, fold):
    half, lanes = (sums.shape[0] // 2, sums.shape[1] // 2)
    sums = sums.astype(bf16)
    block = jnp.concatenate([sums[:, :lanes], sums[:, lanes:], fold], axis=0)
    for axis in (Y_AXIS, X_AXIS):
        block = added(share(block.astype(bf16), axis))
    sums = jnp.concatenate([block[: 2 * half], block[2 * half : 4 * half]], axis=1)
    observed = jnp.concatenate([block[4 * half :, :B], block[4 * half :, B:]], axis=0)
    return (sums, observed)


def weigh(similarity, lookup):
    distance = 2.0 - 2.0 * similarity
    return jnp.exp(-distance / cluster_spread) * lookup


def per_device(counts, batch, seeds, loadings):
    n_cells, n_genes = (lax.axis_size(CELL_AXIS), lax.axis_size(GENE_AXIS))
    n_z, n_core = (lax.axis_size(Z_AXIS), lax.axis_size(CORE_AXIS))
    group, own = (counts.shape[0], batch.shape[0])
    total_cells = group * n_cells
    width = loadings.shape[1]
    mine = K // n_genes
    values = counts.astype(f32)
    shares = dot_rows(jnp.ones((8, counts.shape[1]), bf16), counts.astype(bf16))
    packet = jnp.concatenate([shares[0], batch[:, 0].astype(f32), seeds[:, 0].astype(f32)])
    own_hot = (batch == jnp.arange(B, dtype=jnp.int32)[None, :]).astype(bf16)
    own_twice = jnp.concatenate([own_hot, own_hot], axis=1)
    first = (lax.axis_index(GENE_AXIS) * mine).astype(f32)
    even = lax.axis_index(CORE_AXIS) == 0
    packet, own_twice, first, even = together((packet, own_twice, first, even))
    packets = share(packet, GENE_AXIS)
    depth_total = jnp.sum(packets[:, :group], axis=0)
    labels = packets[:, group:].reshape(n_z, n_core, 2, own).transpose(2, 1, 0, 3)
    group_batch = labels[0].reshape(group)
    group_seeds = labels[1].reshape(group)
    logged = jnp.log1p(10000.0 * values / depth_total[:, None]).astype(bf16)
    partial = dot(logged, loadings)
    batch_hot = hot_columns(group_batch, B)
    batch_twice = jnp.concatenate([batch_hot, batch_hot], axis=0)
    assign = hot_columns(group_seeds - first, mine)
    first_fold = folded(dot_rows(assign, batch_hot))
    group_labels = dot_rows(jnp.ones((8, group), bf16), batch_hot)[0]
    packet = jnp.concatenate([jnp.sum(partial, axis=0), group_labels])
    packet, batch_hot, batch_twice, assign, first_fold = together(
        (packet, batch_hot, batch_twice, assign, first_fold)
    )
    arrived = jnp.sum(share(packet, CELL_AXIS), axis=0)
    center = arrived[:width] / total_cells
    batch_total = arrived[width:][None]
    centred = (partial - center[None]).reshape(n_z, n_core, own, width)
    kept = jnp.where(even, centred[:, 0], centred[:, 1])
    given = jnp.where(even, centred[:, 1], centred[:, 0]).astype(bf16)
    given, kept, batch_total = together((given, kept, batch_total))
    taken = lax.ppermute(given, CORE_AXIS, [(0, 1), (1, 0)])
    pairs = (kept + taken.astype(f32)).astype(bf16)
    embedding = jnp.sum(exchange(pairs, Z_AXIS).astype(f32), axis=0)
    own_rows = unit(embedding)
    unit_rows = gather(share(own_rows, Z_AXIS).reshape(n_z * own, width), CORE_AXIS)
    for iteration in range(ITERS):
        if iteration == 0:
            sums, fold = (dot(assign, unit_rows), first_fold)
        else:
            weights = weigh(dot_rows(rows[:, :width], unit_rows), dot(rows[:, width:], batch_twice))
            norm = jnp.sum(share(jnp.sum(weights, axis=0), GENE_AXIS), axis=0)
            rounded = (weights / norm[None, :]).astype(bf16)
            sums, fold = (dot(rounded, unit_rows), folded(dot_rows(rounded, batch_hot)))
        sums, observed = everywhere(sums, fold)
        penalty = penalty_halves(observed, batch_total, total_cells)
        rows = jnp.concatenate([unit(sums), penalty], axis=1)
    rows = gather(rows, GENE_AXIS)
    weights = weigh(dot_rows(own_rows, rows[:, :width]), dot_rows(own_twice, rows[:, width:]))
    assign = weights / jnp.sum(weights, axis=1, keepdims=True)
    return (embedding, assign, rows[:, :width])


def solution(mesh):
    cells, genes = mesh.devices.shape
    mesh = jax.sharding.Mesh(
        mesh.devices.reshape(cells // X_SIZE, X_SIZE, genes // 2, 2),
        (Y_AXIS, X_AXIS, Z_AXIS, CORE_AXIS),
    )
    owners = P((Y_AXIS, X_AXIS, Z_AXIS, CORE_AXIS), None)
    placed = (P(CELL_AXIS, GENE_AXIS), owners, owners, P(GENE_AXIS, None))
    return jax.shard_map(
        per_device, mesh=mesh, in_specs=placed, out_specs=(owners, owners, P()), check_vma=False
    )
```

profile of v0, /device:TPU:1, one launch (start us, length us, event | category | flops | bytes accessed | tf_op | source)
XLA Modules:
  0.0 160.9 jit_solution(14211592122687259710)
XLA Ops:
  0.6 0.0 copy-start
  0.7 0.0 copy-start.4
  0.7 0.0 copy-start.5
  0.7 1.5 fusion.9
  2.2 0.0 copy-done.4
  2.2 0.0 copy-done.5
  2.2 0.0 copy-start.2
  2.2 0.1 iota_compare_fusion.5
  2.3 0.1 add_convert_fusion.3
  2.4 0.1 concatenate.47
  2.5 19.7 %all_to_all.51 = f32[16,1,1152]{2,1,0:T(1,128)S(1)} all-to-all(f32[16,1,1152]{2,1,0:T(1,128)S(1)} %broadcast_in_dim.27), channel_id=1, replica_groups=mesh['y'=8,'x'=4,'z'=8,'core'=2] {'z','core'}, dimensions={0} | all-to-all | bytes 147456 | tf_op jit(solution)/shard_map/all_to_all | solution.py:25
  22.2 0.1 reshape.107
  22.3 0.1 eq.48
  22.4 0.2 convolution_bitcast_fusion
  22.6 0.1 sub.35
  22.7 0.2 convolution_convert_fusion.3
  22.9 0.1 pad_maximum_fusion.7
  23.0 0.0 copy-done
  23.0 0.0 copy-done.2
  23.0 0.6 fusion.44
  23.7 18.2 %all_to_all.52 = f32[32,1,320]{2,1,0:T(1,128)S(1)} all-to-all(f32[32,1,320]{2,1,0:T(1,128)S(1)} %broadcast_in_dim.29), channel_id=1, replica_groups=mesh['y'=8,'x'=4,'z'=8,'core'=2] {'y','x'}, dimensions={0} | all-to-all | bytes 81920 | tf_op jit(solution)/shard_map/all_to_all | solution.py:25
  42.0 0.1 reduce_sum.110
  42.0 0.1 broadcast_subtract_fusion
  42.1 0.1 fusion.12
  42.2 0.1 select_bitcast_fusion
  42.3 3.4 %collective-permute-start = (bf16[8,64,256]{2,1,0:T(8,128)(2,1)S(1)}, bf16[8,64,256]{2,1,0:T(8,128)(2,1)S(1)}, u32[]{:S(2)}, u32[]{:S(2)}) collective-permute-start(bf16[8,64,256]{2,1,0:T(8,128)(2,1)S(1)} %fusion.12), channel_id=1, source_target_pairs={{0,1},{1,0},{2,3},{3,2},{4,5},{5,4},{6,7},{7,6},{8,9},{9,8},{10,11... | collective-permute-start | bytes 786440 | tf_op jit(solution)/shard_map/ppermute | solution.py:130
  45.6 1.1 collective-permute-done
  46.8 0.1 add_convert_fusion
  46.9 14.7 %all_to_all.53 = bf16[8,64,256]{2,1,0:T(8,128)(2,1)S(1)} all-to-all(bf16[8,64,256]{2,1,0:T(8,128)(2,1)S(1)} %add_convert_fusion), channel_id=1, replica_groups=mesh['y'=8,'x'=4,'z'=8,'core'=2] {'z'}, dimensions={0} | all-to-all | bytes 524288 | tf_op jit(solution)/shard_map/all_to_all | solution.py:25
  61.6 0.0 copy-start.3
  61.6 0.1 multiply_reduce_fusion.2
  61.8 0.1 multiply_convert_fusion.2
  61.8 0.4 copy-done.3
  62.3 14.2 %all_to_all.54 = bf16[8,64,256]{2,1,0:T(8,128)(2,1)S(1)} all-to-all(bf16[8,64,256]{2,1,0:T(8,128)(2,1)S(1)} %broadcast_in_dim.31), channel_id=1, replica_groups=mesh['y'=8,'x'=4,'z'=8,'core'=2] {'z'}, dimensions={0} | all-to-all | bytes 524288 | tf_op jit(solution)/shard_map/all_to_all | solution.py:25
  76.5 2.8 %all_gather.6 = bf16[1024,256]{1,0:T(8,128)(2,1)S(1)} all-gather(bf16[512,256]{1,0:T(8,128)(2,1)S(1)} %bitcast.68), channel_id=1, replica_groups=mesh['y'=8,'x'=4,'z'=8,'core'=2] {'core'}, dimensions={0}, use_global_device_ids=true | all-gather | bytes 786432 | tf_op jit(solution)/shard_map/all_gather | solution.py:33
  79.3 0.2 convolution_convert_fusion.1
  79.6 15.5 %all_to_all.55 = bf16[8,160,128]{2,1,0:T(8,128)(2,1)S(1)} all-to-all(bf16[8,160,128]{2,1,0:T(8,128)(2,1)S(1)} %broadcast_in_dim.32), channel_id=1, replica_groups=mesh['y'=8,'x'=4,'z'=8,'core'=2] {'y'}, dimensions={0} | all-to-all | bytes 655360 | tf_op jit(solution)/shard_map/all_to_all | solution.py:25
  95.2 7.4 %all_to_all.56 = bf16[4,160,128]{2,1,0:T(8,128)(2,1)S(1)} all-to-all(bf16[4,160,128]{2,1,0:T(8,128)(2,1)S(1)} %broadcast_in_dim.34), channel_id=1, replica_groups=mesh['y'=8,'x'=4,'z'=8,'core'=2] {'x'}, dimensions={0} | all-to-all | bytes 327680 | tf_op jit(solution)/shard_map/all_to_all | solution.py:25
  102.6 0.1 fusion.39
  102.7 0.1 multiply_reduce_fusion.1
  102.8 0.3 fusion.7
  103.2 0.1 fusion.23
  103.3 0.1 subtract_convert_fusion.1
  103.4 0.2 fusion.45
  103.7 12.6 %all_to_all.57 = f32[16,1,1024]{2,1,0:T(1,128)S(1)} all-to-all(f32[16,1,1024]{2,1,0:T(1,128)S(1)} %broadcast_in_dim.35), channel_id=1, replica_groups=mesh['y'=8,'x'=4,'z'=8,'core'=2] {'z','core'}, dimensions={0} | all-to-all | bytes 131072 | tf_op jit(solution)/shard_map/all_to_all | solution.py:25
  116.2 0.1 reduce_sum.116
  116.3 0.2 convolution_convert_fusion
  116.5 0.2 convolution_convert_fusion.2
  116.7 0.1 maximum_maximum_fusion
  116.8 16.2 %all_to_all.58 = bf16[8,160,128]{2,1,0:T(8,128)(2,1)S(1)} all-to-all(bf16[8,160,128]{2,1,0:T(8,128)(2,1)S(1)} %broadcast_in_dim.36), channel_id=1, replica_groups=mesh['y'=8,'x'=4,'z'=8,'core'=2] {'y'}, dimensions={0} | all-to-all | bytes 655360 | tf_op jit(solution)/shard_map/all_to_all | solution.py:25
  133.1 7.4 %all_to_all.59 = bf16[4,160,128]{2,1,0:T(8,128)(2,1)S(1)} all-to-all(bf16[4,160,128]{2,1,0:T(8,128)(2,1)S(1)} %broadcast_in_dim.38), channel_id=1, replica_groups=mesh['y'=8,'x'=4,'z'=8,'core'=2] {'x'}, dimensions={0} | all-to-all | bytes 327680 | tf_op jit(solution)/shard_map/all_to_all | solution.py:25
  140.5 0.1 fusion.38
  140.6 0.1 fusion.22
  140.7 0.1 subtract_convert_fusion
  140.8 0.1 multiply_reduce_fusion
  140.9 0.1 multiply_convert_fusion
  141.0 0.1 pad_maximum_fusion.3
  141.1 18.2 %all_gather.7 = bf16[1024,384]{1,0:T(8,128)(2,1)S(1)} all-gather(bf16[64,384]{1,0:T(8,128)(2,1)S(1)} %pad_maximum_fusion.3), channel_id=1, replica_groups=mesh['y'=8,'x'=4,'z'=8,'core'=2] {'z','core'}, dimensions={0}, use_global_device_ids=true | all-gather | bytes 835584 | tf_op jit(solution)/shard_map/all_gather | solution.py:33
  159.3 0.0 copy-start.1
  159.4 0.3 fusion.3
  159.7 0.3 fusion.46
  160.0 0.2 copy-done.1
  160.1 0.8 broadcast_divide_fusion
  (38 shorter events, 0.7 us)
Async XLA Ops:
  0.6 22.4 %copy-start = (bf16[256,256]{1,0:T(8,128)(2,1)S(1)}, bf16[256,256]{1,0:T(8,128)(2,1)}, u32[]{:S(2)}) copy-start(bf16[256,256]{1,0:T(8,128)(2,1)} %param.7) | copy-start | bytes 393220
  0.7 1.5 copy-start.4
  0.7 1.5 copy-start.5
  2.2 20.9 %copy-start.2 = (s32[1024,256]{1,0:T(8,128)S(1)}, s32[1024,256]{1,0:T(8,128)}, u32[]{:S(2)}) copy-start(s32[1024,256]{1,0:T(8,128)} %param.4) | copy-start | bytes 3145732
  42.3 4.5 %collective-permute-start = (bf16[8,64,256]{2,1,0:T(8,128)(2,1)S(1)}, bf16[8,64,256]{2,1,0:T(8,128)(2,1)S(1)}, u32[]{:S(2)}, u32[]{:S(2)}) collective-permute-start(bf16[8,64,256]{2,1,0:T(8,128)(2,1)S(1)} %fusion.12), channel_id=1, source_target_pairs={{0,1},{1,0},{2,3},{3,2},{4,5},{5,4},{6,7},{7,6},{8,9},{9,8},{10,11... | collective-permute-start | bytes 786440 | tf_op jit(solution)/shard_map/ppermute | solution.py:130
  61.6 0.6 copy-start.3
  159.3 0.8 copy-start.1
where the time goes:
time: 161 us
  blocking collectives  147 us (91%)
  matrix products  4.25 us (3%)
  starting transfers between devices  3.36 us (2%)
  other arithmetic  2.81 us (2%)
    all_to_all x9, blocking collectives, exchange(): return lax.all_to_all(blocks, axis, 0, 0, tiled=False)  126 us
    all_gather x2, blocking collectives, gather(): return lax.all_gather(block, axis, tiled=True)  21 us
    ppermute x1, starting transfers between devices, per_device(): taken = lax.ppermute(given, CORE_AXIS, [(0, 1), (1, 0)])  3.36 us
  transfers between devices with their start and end apart: 1, of which 1 were waited for; matrix products, arithmetic and copies ran while one was open for 0% of the time, Pallas kernels for 0%

commit v1 on v0

--- a/solution.py
+++ b/solution.py
@@ -30,7 +30,9 @@
 
 
 def gather(block, axis):
-    return lax.all_gather(block, axis, tiled=True)
+    return jnp.concatenate(
+        lax.all_to_all(jnp.stack([block] * lax.axis_size(axis)), axis, 0, 0), axis=0
+    )
 
 
 def dot(left, right):

time: 161 us -> 173 us (1.075)
  blocking collectives: 147 us -> 158 us
    all_to_all x0 -> x2, blocking collectives: none -> 32 us  [gather(): lax.all_to_all(jnp.stack([block] * lax.axis_size(axis)), axis, 0, 0)]
    all_gather x2 -> x0, blocking collectives: 21 us -> none  [gather(): return lax.all_gather(block, axis, tiled=True)]
where the time goes in v1:
time: 173 us; the launch traced here: 172 us
  blocking collectives  158 us (91%)
  matrix products  4.24 us (2%)
  starting transfers between devices  3.36 us (2%)
  other arithmetic  2.84 us (2%)
    all_to_all x9, blocking collectives, exchange(): return lax.all_to_all(blocks, axis, 0, 0, tiled=False)  126 us
    all_to_all x2, blocking collectives, gather(): lax.all_to_all(jnp.stack([block] * lax.axis_size(axis)), axis, 0, 0)  32 us
  transfers between devices with their start and end apart: 1, of which 1 were waited for; matrix products, arithmetic and copies ran while one was open for 0% of the time, Pallas kernels for 0%

profile of v1, /device:TPU:1, one launch (start us, length us, event | category | flops | bytes accessed | tf_op | source)
XLA Modules:
  0.0 172.0 jit_solution(18075572214896548566)
XLA Ops:
  0.6 0.0 copy-start
  0.7 0.0 copy-start.4
  0.7 0.0 copy-start.5
  0.7 1.5 fusion.9
  2.2 0.0 copy-done.4
  2.2 0.0 copy-done.5
  2.2 0.0 copy-start.2
  2.2 0.1 iota_compare_fusion.5
  2.3 0.1 add_convert_fusion.3
  2.4 0.1 concatenate.47
  2.5 19.7 %all_to_all.61 = f32[16,1,1152]{2,1,0:T(1,128)S(1)} all-to-all(f32[16,1,1152]{2,1,0:T(1,128)S(1)} %broadcast_in_dim.27), channel_id=1, replica_groups=mesh['y'=8,'x'=4,'z'=8,'core'=2] {'z','core'}, dimensions={0} | all-to-all | bytes 147456 | tf_op jit(solution)/shard_map/all_to_all | solution.py:25
  22.2 0.1 reshape.112
  22.3 0.1 eq.48
  22.4 0.2 convolution_bitcast_fusion
  22.6 0.1 sub.35
  22.7 0.2 convolution_convert_fusion.3
  22.9 0.1 pad_maximum_fusion.8
  23.0 0.0 copy-done
  23.0 0.0 copy-done.2
  23.0 0.6 fusion.44
  23.7 18.2 %all_to_all.62 = f32[32,1,320]{2,1,0:T(1,128)S(1)} all-to-all(f32[32,1,320]{2,1,0:T(1,128)S(1)} %broadcast_in_dim.29), channel_id=1, replica_groups=mesh['y'=8,'x'=4,'z'=8,'core'=2] {'y','x'}, dimensions={0} | all-to-all | bytes 81920 | tf_op jit(solution)/shard_map/all_to_all | solution.py:25
  42.0 0.1 reduce_sum.110
  42.0 0.1 broadcast_subtract_fusion
  42.1 0.1 fusion.12
  42.2 0.1 select_bitcast_fusion
  42.3 3.4 %collective-permute-start = (bf16[8,64,256]{2,1,0:T(8,128)(2,1)S(1)}, bf16[8,64,256]{2,1,0:T(8,128)(2,1)S(1)}, u32[]{:S(2)}, u32[]{:S(2)}) collective-permute-start(bf16[8,64,256]{2,1,0:T(8,128)(2,1)S(1)} %fusion.12), channel_id=1, source_target_pairs={{0,1},{1,0},{2,3},{3,2},{4,5},{5,4},{6,7},{7,6},{8,9},{9,8},{10,11... | collective-permute-start | bytes 786440 | tf_op jit(solution)/shard_map/ppermute | solution.py:132
  45.6 1.1 collective-permute-done
  46.8 0.1 add_convert_fusion
  46.9 14.7 %all_to_all.63 = bf16[8,64,256]{2,1,0:T(8,128)(2,1)S(1)} all-to-all(bf16[8,64,256]{2,1,0:T(8,128)(2,1)S(1)} %add_convert_fusion), channel_id=1, replica_groups=mesh['y'=8,'x'=4,'z'=8,'core'=2] {'z'}, dimensions={0} | all-to-all | bytes 524288 | tf_op jit(solution)/shard_map/all_to_all | solution.py:25
  61.6 0.0 copy-start.3
  61.6 0.1 multiply_reduce_fusion.2
  61.8 0.1 multiply_convert_fusion.2
  61.8 0.4 copy-done.3
  62.3 14.2 %all_to_all.64 = bf16[8,64,256]{2,1,0:T(8,128)(2,1)S(1)} all-to-all(bf16[8,64,256]{2,1,0:T(8,128)(2,1)S(1)} %broadcast_in_dim.31), channel_id=1, replica_groups=mesh['y'=8,'x'=4,'z'=8,'core'=2] {'z'}, dimensions={0} | all-to-all | bytes 524288 | tf_op jit(solution)/shard_map/all_to_all | solution.py:25
  76.5 4.8 %all_to_all.65 = bf16[2,512,256]{2,1,0:T(8,128)(2,1)S(1)} all-to-all(bf16[2,512,256]{2,1,0:T(8,128)(2,1)S(1)} %pad_maximum_fusion), channel_id=1, replica_groups=mesh['y'=8,'x'=4,'z'=8,'core'=2] {'core'}, dimensions={0} | all-to-all | bytes 1048576 | tf_op jit(solution)/shard_map/all_to_all | solution.py:34
  81.3 0.2 convolution_convert_fusion.1
  81.6 15.5 %all_to_all.66 = bf16[8,160,128]{2,1,0:T(8,128)(2,1)S(1)} all-to-all(bf16[8,160,128]{2,1,0:T(8,128)(2,1)S(1)} %broadcast_in_dim.32), channel_id=1, replica_groups=mesh['y'=8,'x'=4,'z'=8,'core'=2] {'y'}, dimensions={0} | all-to-all | bytes 655360 | tf_op jit(solution)/shard_map/all_to_all | solution.py:25
  97.2 7.4 %all_to_all.67 = bf16[4,160,128]{2,1,0:T(8,128)(2,1)S(1)} all-to-all(bf16[4,160,128]{2,1,0:T(8,128)(2,1)S(1)} %broadcast_in_dim.34), channel_id=1, replica_groups=mesh['y'=8,'x'=4,'z'=8,'core'=2] {'x'}, dimensions={0} | all-to-all | bytes 327680 | tf_op jit(solution)/shard_map/all_to_all | solution.py:25
  104.6 0.1 fusion.39
  104.7 0.1 multiply_reduce_fusion.1
  104.9 0.3 fusion.7
  105.2 0.1 fusion.23
  105.3 0.1 subtract_convert_fusion.1
  105.4 0.2 fusion.45
  105.7 12.6 %all_to_all.68 = f32[16,1,1024]{2,1,0:T(1,128)S(1)} all-to-all(f32[16,1,1024]{2,1,0:T(1,128)S(1)} %broadcast_in_dim.35), channel_id=1, replica_groups=mesh['y'=8,'x'=4,'z'=8,'core'=2] {'z','core'}, dimensions={0} | all-to-all | bytes 131072 | tf_op jit(solution)/shard_map/all_to_all | solution.py:25
  118.3 0.1 reduce_sum.116
  118.3 0.2 convolution_convert_fusion
  118.5 0.2 convolution_convert_fusion.2
  118.7 0.1 maximum_maximum_fusion
  118.9 16.2 %all_to_all.69 = bf16[8,160,128]{2,1,0:T(8,128)(2,1)S(1)} all-to-all(bf16[8,160,128]{2,1,0:T(8,128)(2,1)S(1)} %broadcast_in_dim.36), channel_id=1, replica_groups=mesh['y'=8,'x'=4,'z'=8,'core'=2] {'y'}, dimensions={0} | all-to-all | bytes 655360 | tf_op jit(solution)/shard_map/all_to_all | solution.py:25
  135.1 7.4 %all_to_all.70 = bf16[4,160,128]{2,1,0:T(8,128)(2,1)S(1)} all-to-all(bf16[4,160,128]{2,1,0:T(8,128)(2,1)S(1)} %broadcast_in_dim.38), channel_id=1, replica_groups=mesh['y'=8,'x'=4,'z'=8,'core'=2] {'x'}, dimensions={0} | all-to-all | bytes 327680 | tf_op jit(solution)/shard_map/all_to_all | solution.py:25
  142.5 0.1 fusion.38
  142.6 0.1 fusion.22
  142.7 0.1 subtract_convert_fusion
  142.8 0.1 multiply_reduce_fusion
  142.9 0.1 multiply_convert_fusion
  143.0 0.1 pad_maximum_fusion.4
  143.1 0.1 stack.5
  143.2 27.2 %all_to_all.71 = bf16[16,64,384]{2,1,0:T(8,128)(2,1)S(1)} all-to-all(bf16[16,64,384]{2,1,0:T(8,128)(2,1)S(1)} %stack.5), channel_id=1, replica_groups=mesh['y'=8,'x'=4,'z'=8,'core'=2] {'z','core'}, dimensions={0} | all-to-all | bytes 1572864 | tf_op jit(solution)/shard_map/all_to_all | solution.py:34
  170.4 0.0 copy-start.1
  170.4 0.3 fusion.3
  170.7 0.3 fusion.46
  171.1 0.2 copy-done.1
  171.2 0.8 broadcast_divide_fusion
  (39 shorter events, 0.7 us)
Async XLA Ops:
  0.6 22.4 %copy-start = (bf16[256,256]{1,0:T(8,128)(2,1)S(1)}, bf16[256,256]{1,0:T(8,128)(2,1)}, u32[]{:S(2)}) copy-start(bf16[256,256]{1,0:T(8,128)(2,1)} %param.7) | copy-start | bytes 393220
  0.7 1.5 copy-start.4
  0.7 1.5 copy-start.5
  2.2 20.9 %copy-start.2 = (s32[1024,256]{1,0:T(8,128)S(1)}, s32[1024,256]{1,0:T(8,128)}, u32[]{:S(2)}) copy-start(s32[1024,256]{1,0:T(8,128)} %param.4) | copy-start | bytes 3145732
  42.3 4.5 %collective-permute-start = (bf16[8,64,256]{2,1,0:T(8,128)(2,1)S(1)}, bf16[8,64,256]{2,1,0:T(8,128)(2,1)S(1)}, u32[]{:S(2)}, u32[]{:S(2)}) collective-permute-start(bf16[8,64,256]{2,1,0:T(8,128)(2,1)S(1)} %fusion.12), channel_id=1, source_target_pairs={{0,1},{1,0},{2,3},{3,2},{4,5},{5,4},{6,7},{7,6},{8,9},{9,8},{10,11... | collective-permute-start | bytes 786440 | tf_op jit(solution)/shard_map/ppermute | solution.py:132
  61.6 0.6 copy-start.3
  170.4 0.8 copy-start.1
